TPU v7x, 32 devices: a whole 2x2x4 slice. The times are simulated.
32 devices in a mesh: row: 2 (over y), col: 16 (over z, x, core).
Axes of the slice: x: 2, y: 2, z: 4, core: 2. Of those that a mesh axis runs over, the one named last changes fastest.
Arguments:
- blocks: float32 [512, 128, 128], P(('row', 'col')), may hold values from -0.3125 to 0.3125
- block_row: int32 [512], P(('row', 'col')), may hold values from 0 to 63, as said below
- block_col: int32 [512], P(('row', 'col')), may hold values from 0 to 63, as said below
- counts: int32 [32], P(('row', 'col')), may hold values from 1 to 16, as said below
- diagonal: float32 [8192], P(('row', 'col')), may hold values from 0.25 to 4
- vector: float32 [8192, 256], P(('row', 'col')), may hold values from -8 to 8
Outputs:
- next_basis: float32 [8192, 256], P(('row', 'col'))
- second_image: float32 [8192, 256], P(('row', 'col'))
- arnoldi_column: float32 [2, 256], replicated
Inputs may be any that keep to these rules, and one draw needn't show every extreme that they name: The slots of device d = r * 16 + c are rows d * 16 to (d + 1) * 16 - 1. Its slot d * 16 + k * 16 + o (k below 1) has block_row // 2 equal to r * 16 + o, and (block_col // 2) % 16 equals c. No pair (block_row, block_col) occurs twice among all slots. `block_col`: paired with block_row as stated there. Only the first counts[d] slots of device d hold blocks; later slots are ignored. Some device has exactly 16.
All inputs are finite; a program needn't handle non-finite values.
Results may differ from a plain program's by a relative error of at most 0.0001.
Values sent between devices are 32-bit elements; how exact they have to be, the bound alone decides.
A program may use at most 64 MiB of HBM per device.

v0:
```python
import math

import jax
import jax.numpy as jnp
from jax import lax
from jax.sharding import PartitionSpec as P


def collect_tiles(products, local_col, live_slot, n_local):
    slot_count = products.shape[0]
    targets = jnp.arange(n_local, dtype=jnp.int32)
    selector = jnp.where(
        (local_col[:, None] == targets[None, :]) & live_slot[:, None], 1.0, 0.0
    ).astype(jnp.float32)
    return jnp.dot(
        selector.T,
        products.reshape(slot_count, -1),
        precision=lax.Precision.HIGHEST,
        preferred_element_type=jnp.float32,
    )


def local_terms(gathered, blocks, local_row, local_col, live_slot, n_local):
    tile_size = blocks.shape[1]
    rhs_count = gathered.shape[1]
    slot_count = blocks.shape[0]
    group_size = math.gcd(slot_count, 32)
    turn_count = slot_count // group_size
    stacked = gathered.reshape(gathered.shape[0] // tile_size, tile_size, rhs_count)

    def advance(turn_id, totals):
        picked = jnp.take(stacked, local_row, axis=0)
        products = jnp.einsum(
            "gab,gak->gbk",
            blocks,
            picked,
            precision=lax.Precision.HIGHEST,
            preferred_element_type=jnp.float32,
        )
        return totals + collect_tiles(products, local_col, live_slot, n_local)

    start_sum = jnp.zeros((n_local, tile_size * rhs_count), jnp.float32)
    return lax.fori_loop(0, turn_count, advance, start_sum)


def per_device(blocks, block_row, block_col, counts, diagonal, vector):
    n_rows = lax.axis_size("row")
    n_cols = lax.axis_size("col")
    tile_size = blocks.shape[1]
    rhs_count = vector.shape[1]
    per_piece = vector.shape[0] // tile_size
    total_rows = vector.shape[0] * n_rows * n_cols
    grid_row = lax.axis_index("row")
    piece_id = block_col // per_piece
    local_col = piece_id // n_cols * per_piece + block_col % per_piece
    live_slot = jnp.arange(blocks.shape[0], dtype=jnp.int32) < counts[0]
    n_local = n_rows * per_piece
    local_row = block_row - grid_row * (n_cols * per_piece)

    def partial_terms(source):
        gathered = lax.all_gather(source, "col", axis=0, tiled=True)
        return local_terms(gathered, blocks, local_row, local_col, live_slot, n_local)

    def apply_transpose(source):
        partial_sums = partial_terms(source).reshape(n_local * tile_size, rhs_count)
        reduced = lax.psum_scatter(partial_sums, "row", scatter_dimension=0, tiled=True)
        return diagonal[:, None] * source + reduced

    squares = lax.psum(jnp.sum(vector * vector, axis=0), ("row", "col"))
    magnitude = jnp.sqrt(squares / total_rows + 1e-06)
    unit_basis = vector / magnitude
    first_image = apply_transpose(unit_basis)
    first_squares, cross_sum, basis_squares = lax.psum(
        (
            jnp.sum(first_image * first_image, axis=0),
            jnp.sum(first_image * unit_basis, axis=0),
            jnp.sum(unit_basis * unit_basis, axis=0),
        ),
        ("row", "col"),
    )
    projection = cross_sum / total_rows
    remainder = first_image - projection * unit_basis
    remainder_power = (
        first_squares - 2.0 * projection * cross_sum + projection * projection * basis_squares
    ) / total_rows
    norm_new = jnp.sqrt(remainder_power + 1e-06)
    next_basis = remainder / norm_new
    second_image = apply_transpose(next_basis)
    return (next_basis, second_image, jnp.stack([projection, norm_new]))


def solution(mesh):
    return jax.shard_map(
        per_device,
        mesh=mesh,
        in_specs=(
            P(("row", "col"), None, None),
            P(("row", "col")),
            P(("row", "col")),
            P(("row", "col")),
            P(("row", "col")),
            P(("row", "col"), None),
        ),
        out_specs=(P(("row", "col"), None), P(("row", "col"), None), P()),
        check_vma=False,
    )
```

profile of v0, /device:TPU:0, one launch (start us, length us, event | category | flops | bytes accessed | tf_op | source)
XLA Modules:
  0.0 259.7 jit_solution(16677184944580297266)
XLA Ops:
  7.2 1.1 multiply_reduce_fusion.3
  8.3 42.0 %psum.28 = f32[256]{0:T(256)S(1)} all-reduce(f32[256]{0:T(256)S(1)} %multiply_reduce_fusion.3), channel_id=1, replica_groups=mesh['row'=2,'col'=16] {'row','col'}, use_global_device_ids=true, to_apply=%region_1.2 | all-reduce | flops 256 | bytes 2048 | tf_op jit(solution)/shard_map/psum | solution.py:69
  50.3 1.7 broadcast_divide_fusion
  52.7 0.7 compare_and_fusion
  53.4 0.7 fusion.32
  54.1 48.3 %all-gather.3.cloned.1.call-done = f32[4096,256]{1,0:T(8,128)} async-done(((f32[256,256]{1,0:T(8,128)}), f32[4096,256]{1,0:T(8,128)}) %all-gather.3.cloned.1.call-update) | async-done | bytes 4194320 | tf_op jit(solution)/shard_map/all_gather | solution.py:61
  102.3 2.9 %gather_fusion = f32[16,128,256]{2,1,0:T(8,128)S(1)} fusion(f32[32,128,256]{2,1,0:T(8,128)} %bitcast.24, s32[1024]{0:T(1024)S(1)} %pad_clamp_fusion), kind=kCustom, calls=%fused_computation.clone | custom fusion | bytes 4194368 | tf_op jit(solution)/shard_map/while/body/eval_jaxpr/jit(_take)/gather | solution.py:32
  105.2 5.2 %fusion.4 = f32[16,128,256]{1,2,0:T(8,128)} fusion(f32[16,128,128]{2,1,0:T(8,128)S(1)} %copy-done, f32[16,128,256]{2,1,0:T(8,128)S(1)} %gather_fusion, pred[16]{0:T(512)(128)(4,1)S(1)} %get-tuple-element.45), kind=kOutput, calls=%fused_computation.6 | convolution fusion | flops 805830656 | bytes 5242896 | tf_op jit(solution)/shard_map/while/body/eval_jaxpr/gab,gak->gbk/dot_general | solution.py:33
  110.4 2.2 copy.15
  112.6 2.0 fusion.16
  114.6 2.2 reshape.42
  116.9 13.3 %reduce-scatter.3.cloned.1.call-done = f32[256,256]{1,0:T(8,128)} async-done(((f32[512,256]{1,0:T(8,128)}), f32[256,256]{1,0:T(8,128)}) %reduce-scatter.3.cloned.1.call-update) | async-done | bytes 262160 | tf_op jit(solution)/shard_map/reduce_scatter | solution.py:66
  130.1 1.1 multiply_reduce_fusion.2
  131.2 39.3 %all-reduce = (f32[256]{0:T(256)S(1)}, f32[256]{0:T(256)S(1)}, f32[256]{0:T(256)S(1)}) all-reduce(f32[256]{0:T(256)S(1)} %get-tuple-element.34, f32[256]{0:T(256)S(1)} %get-tuple-element.33, f32[256]{0:T(256)S(1)} %get-tuple-element.32), channel_id=1, replica_groups=mesh['row'=2,'col'=16] {'row','col'}, use_global_device_ids=true, to_apply=%region_8.10 | all-reduce | flops 768 | bytes 6144 | tf_op jit(solution)/shard_map/psum | solution.py:73
  170.6 1.8 subtract_divide_fusion
  172.6 51.1 %all-gather.5.cloned.1.call-done = f32[4096,256]{1,0:T(8,128)} async-done(((f32[256,256]{1,0:T(8,128)}), f32[4096,256]{1,0:T(8,128)}) %all-gather.5.cloned.1.call-update) | async-done | bytes 4194320 | tf_op jit(solution)/shard_map/all_gather | solution.py:61
  223.6 2.9 %gather_fusion.1 = f32[16,128,256]{2,1,0:T(8,128)S(1)} fusion(f32[32,128,256]{2,1,0:T(8,128)} %bitcast.25, s32[1024]{0:T(1024)S(1)} %pad_clamp_fusion), kind=kCustom, calls=%fused_computation.1.clone | custom fusion | bytes 4194368 | tf_op jit(solution)/shard_map/while/body/eval_jaxpr/jit(_take)/gather | solution.py:32
  226.5 5.2 %fusion.7 = f32[16,128,256]{1,2,0:T(8,128)} fusion(f32[16,128,128]{2,1,0:T(8,128)S(1)} %copy-done, f32[16,128,256]{2,1,0:T(8,128)S(1)} %gather_fusion.1, pred[16]{0:T(512)(128)(4,1)S(1)} %get-tuple-element.45), kind=kOutput, calls=%fused_computation.7 | convolution fusion | flops 805830656 | bytes 5242896 | tf_op jit(solution)/shard_map/while/body/eval_jaxpr/gab,gak->gbk/dot_general | solution.py:33
  231.7 2.2 copy.16
  233.9 2.0 fusion.14
  235.9 2.2 reshape.45
  238.1 0.6 pad_maximum_fusion
  238.7 12.7 %reduce-scatter.5.cloned.1.call-done = f32[256,256]{1,0:T(8,128)} async-done(((f32[512,256]{1,0:T(8,128)}), f32[256,256]{1,0:T(8,128)}) %reduce-scatter.5.cloned.1.call-update) | async-done | bytes 262160 | tf_op jit(solution)/shard_map/reduce_scatter | solution.py:66
  251.4 1.8 multiply_add_fusion
  (20 shorter events, 0.5 us)
Async XLA Ops:
  7.2 98.0 %copy-start = (f32[16,128,128]{2,1,0:T(8,128)S(1)}, f32[16,128,128]{2,1,0:T(8,128)}, u32[]{:S(2)}) copy-start(f32[16,128,128]{2,1,0:T(8,128)} %param.8) | copy-start | bytes 3145732
  7.2 95.1 %all-gather.3.cloned.1.call-start = ((), (), s32[]{:S(2)}) async-start(), calls=%async_computation.2 | async-start | bytes 4456448 | tf_op jit(solution)/shard_map/all_gather | solution.py:61
  52.0 78.1 %reduce-scatter.3.cloned.1.call-start = ((), (), s32[]{:S(2)}) async-start(), calls=%async_computation.3 | async-start | bytes 786432 | tf_op jit(solution)/shard_map/reduce_scatter | solution.py:66
  112.6 17.6 %copy-start.1 = (f32[256,256]{1,0:T(8,128)S(1)}, f32[256,256]{1,0:T(8,128)}, u32[]{:S(2)}) copy-start(f32[256,256]{1,0:T(8,128)} %param.13) | copy-start | bytes 786436
  112.6 17.6 %copy-start.3 = (f32[256]{0:T(256)S(1)}, f32[256]{0:T(256)}, u32[]{:S(2)}) copy-start(f32[256]{0:T(256)} %param.12) | copy-start | bytes 3076
  116.8 106.8 %all-gather.5.cloned.1.call-start = ((), (), s32[]{:S(2)}) async-start(), calls=%async_computation.4 | async-start | bytes 4456448 | tf_op jit(solution)/shard_map/all_gather | solution.py:61
  172.4 79.1 %reduce-scatter.5.cloned.1.call-start = ((), (), s32[]{:S(2)}) async-start(), calls=%async_computation.5 | async-start | bytes 786432 | tf_op jit(solution)/shard_map/reduce_scatter | solution.py:66
  233.9 17.5 %copy-start.2 = (f32[256,256]{1,0:T(8,128)S(1)}, f32[256,256]{1,0:T(8,128)}, u32[]{:S(2)}) copy-start(f32[256,256]{1,0:T(8,128)} %subtract_divide_fusion) | copy-start | bytes 786436
Sparse Core Ops, SparseCore 0:
  52.1 50.1 all-gather.2
  116.9 13.1 reduce-scatter.2
  172.5 51.1 all-gather.4
  238.2 13.1 reduce-scatter.4
where the time goes:
time: 260 us
  waiting for transfers between devices  125 us (48%)
  blocking collectives  81.3 us (31%)
  local copies, waits for them, and re-layouts  14.5 us (6%)
  between operations  14.5 us (6%)
  matrix products  14.3 us (6%)
  other arithmetic  9.32 us (4%)
    all_gather x2, waiting for transfers between devices, partial_terms(): gathered = lax.all_gather(source, 'col', axis=0, tiled=True)  99.3 us
    psum x1, blocking collectives, per_device(): squares = lax.psum(jnp.sum(vector * vector, axis=0), ('row', 'col'))  42 us
    psum x1, blocking collectives, per_device(): lax.psum((jnp.sum(first_image * first_image, axis=0), jnp.sum(first_image...  39.3 us
    reduce_scatter x2, waiting for transfers between devices, apply_transpose(): lax.psum_scatter(partial_sums, 'row', scatter_dimension=0, tiled=True)  26 us
    dot_general x2, matrix products, advance(): jnp.einsum('gab,gak->gbk', blocks, picked, precision=lax.Precision.HIGHES...  10.3 us
    gather x2, local copies, waits for them, and re-layouts, advance(): picked = jnp.take(stacked, local_row, axis=0)  5.73 us
  transfers between devices with their start and end apart: 4, of which 4 were waited for; matrix products, arithmetic and copies ran while one was open for 1% of the time, Pallas kernels for 0%

commit v1 on v0

v1 whole, which is shorter than its diff:
```python
import functools

import jax
import jax.numpy as jnp
from jax import lax
from jax.experimental import pallas as pl
from jax.experimental.pallas import tpu as pltpu
from jax.sharding import PartitionSpec as P

MESH = pl.DeviceIdType.MESH
LANES = 128
STAT_ROWS = 8


def chip_grid(chips):
    x = max(d for d in range(1, chips + 1) if chips % d == 0 and d * d <= chips)
    return chips // x, x


def nearest(turn, here, size):
    both = jnp.minimum(here, size - 1 - here)
    reach = (turn + 1) // 2
    near = jnp.where(turn % 2 == 1, here + reach, here - reach)
    far = jnp.where(here < size - 1 - here, turn, size - 1 - turn)
    return jnp.where(turn <= 2 * both, near, far)


def split(value):
    high = value.astype(jnp.bfloat16)
    low = (value - high.astype(jnp.float32)).astype(jnp.bfloat16)
    return high, low


def kernel(
    n_rows, n_cols, total_rows,
    brow, bcol, counts, blocks_hbm, diag_ref, vec_hbm,
    next_ref, second_ref, column_ref,
    blocks, held, w_high, w_low, totals, partner, diag, stat_col, stat_row,
    local_sem, unit_send, unit_recv, y_send, y_recv, col_send, col_recv, row_send, row_recv,
):
    tile = blocks.shape[1]
    slots = blocks.shape[0]
    cap = slots // n_cols
    per = held.shape[3]
    halves = held.shape[1]
    n_local = n_rows * per
    chips = n_cols // 2
    size_z, size_x = chip_grid(chips)
    row, col = lax.axis_index("row"), lax.axis_index("col")
    core, chip = col % 2, col // 2
    at_x, at_z = chip % size_x, chip // size_x

    own = []
    for h in range(halves):
        for b in range(per):
            own.append(pltpu.make_async_copy(
                vec_hbm.at[pl.ds(b * tile, tile), pl.ds(h * LANES, LANES)],
                held.at[0, h, col, b], local_sem.at[h * per + b]))
    own.append(pltpu.make_async_copy(blocks_hbm, blocks, local_sem.at[halves * per]))
    for copy in own:
        copy.start()

    barrier = pltpu.get_barrier_semaphore()

    @pl.loop(1, n_cols)
    def _(step):
        pl.semaphore_signal(barrier, inc=1, device_id=(row, (col + step) % n_cols), device_id_type=MESH)

    @pl.loop(1, n_rows)
    def _(step):
        pl.semaphore_signal(barrier, inc=1, device_id=((row + step) % n_rows, col), device_id_type=MESH)

    pl.semaphore_wait(barrier, n_cols + n_rows - 2)

    def branches(g, h, sx, sz, act):
        source_chip = sz * size_x + sx
        source = source_chip * 2 + core
        if halves > 1 and h == halves - 1:
            x_first = (sz == 0) | (sz == size_z - 1)
        else:
            x_first = sz < 0
        along_z = x_first | (at_x == sx)
        along_x = jnp.logical_not(x_first) | (at_z == sz)
        targets = (
            (along_z & (at_z >= sz) & (at_z + 1 < size_z), at_x, at_z + 1, core),
            (along_z & (at_z <= sz) & (at_z >= 1), at_x, at_z - 1, core),
            (along_x & (at_x >= sx) & (at_x + 1 < size_x), at_x + 1, at_z, core),
            (along_x & (at_x <= sx) & (at_x >= 1), at_x - 1, at_z, core),
            (None, at_x, at_z, 1 - core),
        )
        piece = held.at[g, h, source]
        for i, (wanted, tx, tz, tcore) in enumerate(targets):
            def go(i=i, tx=tx, tz=tz, tcore=tcore):
                act(pltpu.make_async_remote_copy(
                    piece, piece, unit_send.at[g, h, source_chip, i], unit_recv.at[g, h, source],
                    device_id=(row, (tz * size_x + tx) * 2 + tcore), device_id_type=MESH))
            if wanted is None:
                go()
            else:
                pl.when(wanted)(go)

    def start(copy):
        copy.start()

    def drain(copy):
        copy.wait_send()

    def arrived(g, h, source):
        piece = held.at[g, h, source]
        pltpu.make_async_remote_copy(
            piece, piece, unit_send.at[g, h, 0, 0], unit_recv.at[g, h, source],
            device_id=(row, col), device_id_type=MESH).wait_recv()

    def send_own(g, h):
        branches(g, h, at_x, at_z, start)

    def multiply(g, h, p):
        parts = []
        for q in range(cap):
            for kk in range(2):
                o = p * 2 + kk
                which = brow[q * n_cols + o] % per
                part = held[g, h, o, 0]
                for b in range(1, per):
                    part = jnp.where(which == b, held[g, h, o, b], part)
                parts.append(part)
        high, low = split(jnp.concatenate(parts, axis=0))
        dot = functools.partial(jnp.dot, preferred_element_type=jnp.float32)
        product = dot(w_high[p], high) + dot(w_high[p], low) + dot(w_low[p], high)
        return product.reshape(n_rows, per, tile, LANES)

    def first_turn(g, h):
        arrived(g, h, chip * 2 + 1 - core)
        totals[h] = multiply(g, h, chip)

    def turns(g, h, low, high):
        @pl.loop(low, high)
        def _(turn):
            sz = nearest(turn // size_x, at_z, size_z)
            sx = nearest(turn % size_x, at_x, size_x)
            p = sz * size_x + sx
            arrived(g, h, p * 2 + core)
            branches(g, h, sx, sz, start)
            arrived(g, h, p * 2 + 1 - core)
            totals[h] += multiply(g, h, p)

    def y_copy(g, h, step):
        target = (row + step) % n_rows
        return pltpu.make_async_remote_copy(
            totals.at[h, target], partner.at[g, h, row], y_send.at[g, h, step - 1], y_recv.at[g, h, step - 1],
            device_id=(target, col), device_id_type=MESH)

    def y_start(g, h):
        for step in range(1, n_rows):
            y_copy(g, h, step).start()

    def y_drain(g, h):
        for step in range(1, n_rows):
            y_copy(g, h, step).wait_send()

    def y_sum(g, h):
        total = totals[h, row]
        for step in range(1, n_rows):
            origin = (row + n_rows - step) % n_rows
            pltpu.make_async_remote_copy(
                totals.at[h, row], partner.at[g, h, origin], y_send.at[g, h, step - 1], y_recv.at[g, h, step - 1],
                device_id=(row, col), device_id_type=MESH).wait_recv()
            total = total + partner[g, h, origin]
        return total

    def stats_begin(i, rows):
        filler = jnp.zeros((STAT_ROWS - len(rows), LANES), jnp.float32)
        stat_col[i, col] = jnp.concatenate(list(rows) + [filler], axis=0)

        @pl.loop(1, n_cols)
        def _(step):
            pltpu.make_async_remote_copy(
                stat_col.at[i, col], stat_col.at[i, col], col_send.at[i], col_recv.at[i],
                device_id=(row, (col + step) % n_cols), device_id_type=MESH).start()

    def stats_turn(i):
        many = stat_col.at[i, pl.ds(0, n_cols - 1)]
        pltpu.make_async_copy(many, many, col_recv.at[i]).wait()
        stat_row[i, row] = jnp.sum(stat_col[i], axis=0)

        @pl.loop(1, n_rows)
        def _(step):
            pltpu.make_async_remote_copy(
                stat_row.at[i, row], stat_row.at[i, row], row_send.at[i], row_recv.at[i],
                device_id=((row + step) % n_rows, col), device_id_type=MESH).start()

    def stats_end(i):
        many = stat_row.at[i, pl.ds(0, n_rows - 1)]
        pltpu.make_async_copy(many, many, row_recv.at[i]).wait()
        return jnp.sum(stat_row[i], axis=0)

    def stats_drain(i):
        many = stat_col.at[i, pl.ds(0, n_cols - 1)]
        pltpu.make_async_copy(many, many, col_send.at[i]).wait()
        many = stat_row.at[i, pl.ds(0, n_rows - 1)]
        pltpu.make_async_copy(many, many, row_send.at[i]).wait()

    def over_rows(value):
        return jnp.sum(value.reshape(per * tile, LANES), axis=0, keepdims=True)

    for copy in own[:-1]:
        copy.wait()
    send_own(0, 0)
    squares = []
    for h in range(halves):
        mine = held[0, h, col]
        squares.append(over_rows(mine * mine))
    stats_begin(0, squares)
    for b in range(per):
        diag[b] = jnp.broadcast_to(diag_ref[pl.ds(b, 1), :], (tile, LANES)).T
    own[-1].wait()

    @pl.loop(0, chips)
    def _(p):
        for q in range(cap):
            for kk in range(2):
                local = p * 2 + kk
                slot = q * n_cols + local
                piece = bcol[slot] // per
                target = piece // n_cols * per + bcol[slot] % per
                target = jnp.where(slot < counts[0], target, -1)
                high, low = split(blocks[slot].T)
                at = pl.ds((q * 2 + kk) * tile, tile)
                for j in range(n_local):
                    keep = jnp.where(target == j, 1.0, 0.0).astype(jnp.bfloat16)
                    w_high[p, pl.ds(j * tile, tile), at] = high * keep
                    w_low[p, pl.ds(j * tile, tile), at] = low * keep

    middle = max(1, chips // 2)
    magnitude, image_rows = [], []
    for g in range(2):
        for h in range(halves):
            if g == 1:
                y_drain(0, h)
            first_turn(g, h)
            turns(g, h, 1, middle)
            last = (g, h - 1) if h else (g - 1, halves - 1)
            if (g, h) == (0, 0):
                stats_turn(0)
            elif last[0] == 0:
                lh = last[1]
                if not magnitude:
                    total_squares = stats_end(0)
                    magnitude = [jnp.sqrt(total_squares[k:k + 1] / total_rows + 1e-06) for k in range(halves)]
                mine = held[0, lh, col]
                image = (diag[...] * mine + y_sum(0, lh)) / magnitude[lh]
                held[1, lh, col] = image
                send_own(1, lh)
                image_rows.append(over_rows(image * image))
                image_rows.append(over_rows(image * (mine / magnitude[lh])))
                if len(image_rows) == 2 * halves:
                    stats_begin(1, image_rows)
            else:
                if h == 1:
                    stats = stats_end(1)
                    projection, norm_new = [], []
                    for k in range(halves):
                        image_squares, cross = stats[2 * k:2 * k + 1], stats[2 * k + 1:2 * k + 2]
                        basis_squares = total_squares[k:k + 1] / (magnitude[k] * magnitude[k])
                        part = cross / total_rows
                        power = (image_squares - 2.0 * part * cross + part * part * basis_squares) / total_rows
                        projection.append(part)
                        norm_new.append(jnp.sqrt(jnp.maximum(power, 0.0) + 1e-06))
                        at = pl.ds(k * LANES, LANES)
                        image = held[1, k, col].reshape(per * tile, LANES)
                        basis = held[0, k, col].reshape(per * tile, LANES) / magnitude[k]
                        next_ref[:, at] = (image - part * basis) / norm_new[k]
                        column_ref[pl.ds(0, 1), at] = part
                        column_ref[pl.ds(1, 1), at] = norm_new[k]
                finish(g, last[1], held, diag, projection, norm_new, y_sum, second_ref, col)
            if g == 0 and h + 1 < halves:
                send_own(0, h + 1)
            turns(g, h, middle, chips)
            y_start(g, h)
            if (g, h) == (1, 0):
                stats_turn(1)
    finish(1, halves - 1, held, diag, projection, norm_new, y_sum, second_ref, col)

    for g in range(2):
        stats_drain(g)
        for h in range(halves):
            if g == 1:
                y_drain(g, h)

            @pl.loop(0, chips)
            def _(p):
                branches(g, h, p % size_x, p // size_x, drain)


def finish(g, h, held, diag, projection, norm_new, y_sum, second_ref, col):
    image = held[g, h, col]
    result = (diag[...] * image + y_sum(g, h) - projection[h] * image) / norm_new[h]
    second_ref[:, pl.ds(h * LANES, LANES)] = result.reshape(second_ref.shape[0], LANES)


def per_device(blocks, block_row, block_col, counts, diagonal, vector):
    n_rows, n_cols = lax.axis_size("row"), lax.axis_size("col")
    slots, tile, _ = blocks.shape
    mine, rhs = vector.shape
    per, halves = mine // tile, rhs // LANES
    cap, chips, n_local = slots // n_cols, n_cols // 2, n_rows * per
    smem = pl.BlockSpec(memory_space=pltpu.SMEM)
    vmem = pl.BlockSpec(memory_space=pltpu.VMEM)
    anywhere = pl.BlockSpec(memory_space=pl.ANY)
    f32, dma = jnp.float32, pltpu.SemaphoreType.DMA
    weight = pltpu.VMEM((chips, n_local * tile, 2 * cap * tile), jnp.bfloat16)
    return pl.pallas_call(
        functools.partial(kernel, n_rows, n_cols, mine * n_rows * n_cols),
        out_shape=(
            jax.ShapeDtypeStruct((mine, rhs), f32),
            jax.ShapeDtypeStruct((mine, rhs), f32),
            jax.ShapeDtypeStruct((2, rhs), f32),
        ),
        in_specs=[smem, smem, smem, anywhere, vmem, anywhere],
        out_specs=(vmem, vmem, vmem),
        scratch_shapes=[
            pltpu.VMEM((slots, tile, tile), f32),
            pltpu.VMEM((2, halves, n_cols, per, tile, LANES), f32),
            weight,
            weight,
            pltpu.VMEM((halves, n_rows, per, tile, LANES), f32),
            pltpu.VMEM((2, halves, n_rows, per, tile, LANES), f32),
            pltpu.VMEM((per, tile, LANES), f32),
            pltpu.VMEM((2, n_cols, STAT_ROWS, LANES), f32),
            pltpu.VMEM((2, n_rows, STAT_ROWS, LANES), f32),
            dma((halves * per + 1,)),
            dma((2, halves, chips, 5)),
            dma((2, halves, n_cols)),
            dma((2, halves, n_rows)),
            dma((2, halves, n_rows)),
            dma((2,)), dma((2,)), dma((2,)), dma((2,)),
        ],
        compiler_params=pltpu.CompilerParams(
            collective_id=0, has_side_effects=True, vmem_limit_bytes=60 * 1024 * 1024),
    )(block_row, block_col, counts, blocks, diagonal.reshape(per, tile), vector)


def solution(mesh):
    spec = P(("row", "col"))
    return jax.shard_map(
        per_device,
        mesh=mesh,
        in_specs=(P(("row", "col"), None, None), spec, spec, spec, spec, P(("row", "col"), None)),
        out_specs=(P(("row", "col"), None), P(("row", "col"), None), P()),
        check_vma=False,
    )
```

time: 260 us -> 120 us (0.46)
  the two profiles are of different devices: /device:TPU:0 before, /device:TPU:26 now
where the time goes in v1:
time: 120 us
  Pallas kernels  115 us (96%)
  local copies, waits for them, and re-layouts  3 us (2%)
  between operations  1.3 us (1%)
    pallas_call x1, Pallas kernels, per_device(): pl.pallas_call(functools.partial(kernel, n_rows, n_cols, mine * n_rows *...  115 us
    unnamed x7, local copies, waits for them, and re-layouts  3 us

profile of v1, /device:TPU:26, one launch (start us, length us, event | category | flops | bytes accessed | tf_op | source)
XLA Modules:
  0.0 119.8 jit_solution(10329385588142308556)
XLA Ops:
  1.3 115.5 %shard_map.85 = (f32[256,256]{1,0:T(8,128)}, f32[256,256]{1,0:T(8,128)}, f32[2,256]{1,0:T(2,128)}) custom-call(s32[16]{0:T(128)} %brow.1, s32[16]{0:T(128)} %bcol.1, s32[1]{0:T(128)S(6)} %copy.12.counts, f32[16,128,128]{2,1,0:T(8,128)} %blocks_hbm.1, f32[2,128]{1,0:T(2,128)} %bitcast.1, f32[256,256]{1,0:T(8,128)} %vec_hbm.1), custom_call_target="tpu_custom_call" | custom-call | tf_op jit(solution)/shard_map/pallas_call | solution.py:312
  116.7 0.0 copy-start
  116.8 1.7 %copy.13 = f32[256,256]{1,0:T(8,128)} copy(f32[256,256]{1,0:T(8,128)} %get-tuple-element.6) | data formatting | bytes 524288
  118.5 0.0 copy-done
  118.5 0.0 copy-start.1
  118.5 0.7 copy.14
  119.2 0.0 copy-done.1
  119.2 0.6 copy.15
Async XLA Ops:
  116.7 1.7 %copy-start = (f32[256,256]{1,0:T(8,128)S(1)}, f32[256,256]{1,0:T(8,128)}, u32[]{:S(2)}) copy-start(f32[256,256]{1,0:T(8,128)} %get-tuple-element.7) | copy-start | bytes 786436
  118.5 0.7 copy-start.1

commit v2 on v1

--- a/solution.py
+++ b/solution.py
@@ -9,6 +9,7 @@
 
 MESH = pl.DeviceIdType.MESH
 LANES = 128
+CUTS = 1
 STAT_ROWS = 8
 
 
@@ -36,7 +37,7 @@
     brow, bcol, counts, blocks_hbm, diag_ref, vec_hbm,
     next_ref, second_ref, column_ref,
     blocks, held, w_high, w_low, totals, partner, diag, stat_col, stat_row,
-    local_sem, unit_send, unit_recv, y_send, y_recv, col_send, col_recv, row_send, row_recv,
+    local_sem, unit_send, unit_recv, pair_send, pair_recv, y_send, y_recv, col_send, col_recv, row_send, row_recv,
 ):
     tile = blocks.shape[1]
     slots = blocks.shape[0]
@@ -72,7 +73,10 @@
 
     pl.semaphore_wait(barrier, n_cols + n_rows - 2)
 
-    def branches(g, h, sx, sz, act):
+    def cut(g, h, source, part):
+        return held.at[g, h, source, part // CUTS, pl.ds(part % CUTS * (tile // CUTS), tile // CUTS)]
+
+    def branches(g, h, sx, sz, act, part):
         source_chip = sz * size_x + sx
         source = source_chip * 2 + core
         if halves > 1 and h == halves - 1:
@@ -86,18 +90,21 @@
             (along_z & (at_z <= sz) & (at_z >= 1), at_x, at_z - 1, core),
             (along_x & (at_x >= sx) & (at_x + 1 < size_x), at_x + 1, at_z, core),
             (along_x & (at_x <= sx) & (at_x >= 1), at_x - 1, at_z, core),
-            (None, at_x, at_z, 1 - core),
         )
-        piece = held.at[g, h, source]
+        piece = cut(g, h, source, part)
         for i, (wanted, tx, tz, tcore) in enumerate(targets):
             def go(i=i, tx=tx, tz=tz, tcore=tcore):
                 act(pltpu.make_async_remote_copy(
-                    piece, piece, unit_send.at[g, h, source_chip, i], unit_recv.at[g, h, source],
+                    piece, piece, unit_send.at[g, h, source_chip, part, i], unit_recv.at[g, h, source, part],
                     device_id=(row, (tz * size_x + tx) * 2 + tcore), device_id_type=MESH))
-            if wanted is None:
-                go()
-            else:
-                pl.when(wanted)(go)
+            pl.when(wanted)(go)
+
+    def share(g, h, source_chip, act):
+        source = source_chip * 2 + core
+        piece = held.at[g, h, source]
+        act(pltpu.make_async_remote_copy(
+            piece, piece, pair_send.at[g, h, source_chip], pair_recv.at[g, h, source_chip],
+            device_id=(row, chip * 2 + 1 - core), device_id_type=MESH))
 
     def start(copy):
         copy.start()
@@ -105,14 +112,22 @@
     def drain(copy):
         copy.wait_send()
 
-    def arrived(g, h, source):
-        piece = held.at[g, h, source]
+    def arrived(g, h, source, part):
+        piece = cut(g, h, source, part)
         pltpu.make_async_remote_copy(
-            piece, piece, unit_send.at[g, h, 0, 0], unit_recv.at[g, h, source],
+            piece, piece, unit_send.at[g, h, 0, part, 0], unit_recv.at[g, h, source, part],
             device_id=(row, col), device_id_type=MESH).wait_recv()
 
+    def shared(g, h, source_chip):
+        piece = held.at[g, h, source_chip * 2 + 1 - core]
+        pltpu.make_async_remote_copy(
+            piece, piece, pair_send.at[g, h, source_chip], pair_recv.at[g, h, source_chip],
+            device_id=(row, col), device_id_type=MESH).wait_recv()
+
     def send_own(g, h):
-        branches(g, h, at_x, at_z, start)
+        for part in range(per * CUTS):
+            branches(g, h, at_x, at_z, start, part)
+        share(g, h, chip, start)
 
     def multiply(g, h, p):
         parts = []
@@ -129,20 +144,37 @@
         product = dot(w_high[p], high) + dot(w_high[p], low) + dot(w_low[p], high)
         return product.reshape(n_rows, per, tile, LANES)
 
-    def first_turn(g, h):
-        arrived(g, h, chip * 2 + 1 - core)
-        totals[h] = multiply(g, h, chip)
-
-    def turns(g, h, low, high):
+    def place(turn):
+        return nearest(turn // size_x, at_z, size_z), nearest(turn % size_x, at_x, size_x)
+
+    def relay(g, h, turn):
+        sz, sx = place(turn)
+        p = sz * size_x + sx
+        for part in range(per * CUTS):
+            arrived(g, h, p * 2 + core, part)
+            branches(g, h, sx, sz, start, part)
+        share(g, h, p, start)
+
+    def consume(g, h, turn):
+        sz, sx = place(turn)
+        p = sz * size_x + sx
+        shared(g, h, p)
+        totals[h] += multiply(g, h, p)
+
+    def turns(low, high, *phases):
         @pl.loop(low, high)
         def _(turn):
-            sz = nearest(turn // size_x, at_z, size_z)
-            sx = nearest(turn % size_x, at_x, size_x)
-            p = sz * size_x + sx
-            arrived(g, h, p * 2 + core)
-            branches(g, h, sx, sz, start)
-            arrived(g, h, p * 2 + 1 - core)
-            totals[h] += multiply(g, h, p)
+            for g, h, shift in phases:
+                relay(g, h, turn + shift)
+            for g, h, shift in phases:
+                consume(g, h, turn + shift - 1)
+
+    def clear(h):
+        totals[h] = jnp.zeros_like(totals[h])
+
+    def close(g, h):
+        consume(g, h, chips - 1)
+        y_start(g, h)
 
     def y_copy(g, h, step):
         target = (row + step) % n_rows
@@ -206,6 +238,7 @@
     for copy in own[:-1]:
         copy.wait()
     send_own(0, 0)
+    send_own(0, 1)
     squares = []
     for h in range(halves):
         mine = held[0, h, col]
@@ -231,65 +264,75 @@
                     w_high[p, pl.ds(j * tile, tile), at] = high * keep
                     w_low[p, pl.ds(j * tile, tile), at] = low * keep
 
-    middle = max(1, chips // 2)
-    magnitude, image_rows = [], []
-    for g in range(2):
-        for h in range(halves):
-            if g == 1:
-                y_drain(0, h)
-            first_turn(g, h)
-            turns(g, h, 1, middle)
-            last = (g, h - 1) if h else (g - 1, halves - 1)
-            if (g, h) == (0, 0):
-                stats_turn(0)
-            elif last[0] == 0:
-                lh = last[1]
-                if not magnitude:
-                    total_squares = stats_end(0)
-                    magnitude = [jnp.sqrt(total_squares[k:k + 1] / total_rows + 1e-06) for k in range(halves)]
-                mine = held[0, lh, col]
-                image = (diag[...] * mine + y_sum(0, lh)) / magnitude[lh]
-                held[1, lh, col] = image
-                send_own(1, lh)
-                image_rows.append(over_rows(image * image))
-                image_rows.append(over_rows(image * (mine / magnitude[lh])))
-                if len(image_rows) == 2 * halves:
-                    stats_begin(1, image_rows)
-            else:
-                if h == 1:
-                    stats = stats_end(1)
-                    projection, norm_new = [], []
-                    for k in range(halves):
-                        image_squares, cross = stats[2 * k:2 * k + 1], stats[2 * k + 1:2 * k + 2]
-                        basis_squares = total_squares[k:k + 1] / (magnitude[k] * magnitude[k])
-                        part = cross / total_rows
-                        power = (image_squares - 2.0 * part * cross + part * part * basis_squares) / total_rows
-                        projection.append(part)
-                        norm_new.append(jnp.sqrt(jnp.maximum(power, 0.0) + 1e-06))
-                        at = pl.ds(k * LANES, LANES)
-                        image = held[1, k, col].reshape(per * tile, LANES)
-                        basis = held[0, k, col].reshape(per * tile, LANES) / magnitude[k]
-                        next_ref[:, at] = (image - part * basis) / norm_new[k]
-                        column_ref[pl.ds(0, 1), at] = part
-                        column_ref[pl.ds(1, 1), at] = norm_new[k]
-                finish(g, last[1], held, diag, projection, norm_new, y_sum, second_ref, col)
-            if g == 0 and h + 1 < halves:
-                send_own(0, h + 1)
-            turns(g, h, middle, chips)
-            y_start(g, h)
-            if (g, h) == (1, 0):
-                stats_turn(1)
-    finish(1, halves - 1, held, diag, projection, norm_new, y_sum, second_ref, col)
+    half = chips // 2
+    rest = min(chips, chips - half + 1)
+    late = max(rest, chips - 1)
+    clear(0)
+    clear(1)
+    turns(1, half, (0, 0, 0))
+    turns(half, chips, (0, 0, 0), (0, 1, 1 - half))
+    close(0, 0)
+    stats_turn(0)
+    turns(rest, late, (0, 1, 0))
+    total_squares = stats_end(0)
+    magnitude = [jnp.sqrt(total_squares[k:k + 1] / total_rows + 1e-06) for k in range(2)]
+    image_rows = []
+
+    def make_image(h):
+        mine = held[0, h, col]
+        image = (diag[...] * mine + y_sum(0, h)) / magnitude[h]
+        held[1, h, col] = image
+        send_own(1, h)
+        image_rows.append(over_rows(image * image))
+        image_rows.append(over_rows(image * (mine / magnitude[h])))
+
+    make_image(0)
+    y_drain(0, 0)
+    clear(0)
+    turns(late, chips, (0, 1, 0))
+    close(0, 1)
+    early = min(3, half)
+    turns(1, early, (1, 0, 0))
+    make_image(1)
+    stats_begin(1, image_rows)
+    y_drain(0, 1)
+    clear(1)
+    turns(early, half, (1, 0, 0))
+    turns(half, chips, (1, 0, 0), (1, 1, 1 - half))
+    close(1, 0)
+    stats_turn(1)
+    turns(rest, late, (1, 1, 0))
+    stats = stats_end(1)
+    projection, norm_new = [], []
+    for k in range(2):
+        image_squares, cross = stats[2 * k:2 * k + 1], stats[2 * k + 1:2 * k + 2]
+        basis_squares = total_squares[k:k + 1] / (magnitude[k] * magnitude[k])
+        part = cross / total_rows
+        power = (image_squares - 2.0 * part * cross + part * part * basis_squares) / total_rows
+        projection.append(part)
+        norm_new.append(jnp.sqrt(jnp.maximum(power, 0.0) + 1e-06))
+        at = pl.ds(k * LANES, LANES)
+        image = held[1, k, col].reshape(per * tile, LANES)
+        basis = held[0, k, col].reshape(per * tile, LANES) / magnitude[k]
+        next_ref[:, at] = (image - part * basis) / norm_new[k]
+        column_ref[pl.ds(0, 1), at] = part
+        column_ref[pl.ds(1, 1), at] = norm_new[k]
+    finish(1, 0, held, diag, projection, norm_new, y_sum, second_ref, col)
+    turns(late, chips, (1, 1, 0))
+    close(1, 1)
+    finish(1, 1, held, diag, projection, norm_new, y_sum, second_ref, col)
 
     for g in range(2):
         stats_drain(g)
-        for h in range(halves):
+        for h in range(2):
             if g == 1:
                 y_drain(g, h)
 
             @pl.loop(0, chips)
             def _(p):
-                branches(g, h, p % size_x, p // size_x, drain)
+                for part in range(per * CUTS):
+                    branches(g, h, p % size_x, p // size_x, drain, part)
+                share(g, h, p, drain)
 
 
 def finish(g, h, held, diag, projection, norm_new, y_sum, second_ref, col):
@@ -329,8 +372,10 @@
             pltpu.VMEM((2, n_cols, STAT_ROWS, LANES), f32),
             pltpu.VMEM((2, n_rows, STAT_ROWS, LANES), f32),
             dma((halves * per + 1,)),
-            dma((2, halves, chips, 5)),
-            dma((2, halves, n_cols)),
+            dma((2, halves, chips, per * CUTS, 4)),
+            dma((2, halves, n_cols, per * CUTS)),
+            dma((2, halves, chips)),
+            dma((2, halves, chips)),
             dma((2, halves, n_rows)),
             dma((2, halves, n_rows)),
             dma((2,)), dma((2,)), dma((2,)), dma((2,)),

time: 120 us -> 87.9 us (0.73)
  the two profiles are of different devices: /device:TPU:26 before, /device:TPU:0 now
where the time goes in v2:
time: 87.9 us; the launch traced here: 87.7 us
  Pallas kernels  83.4 us (95%)
  local copies, waits for them, and re-layouts  3 us (3%)
  between operations  1.3 us (1%)
    pallas_call x1, Pallas kernels, per_device(): pl.pallas_call(functools.partial(kernel, n_rows, n_cols, mine * n_rows *...  83.4 us
    unnamed x7, local copies, waits for them, and re-layouts  3 us

profile of v2, /device:TPU:0, one launch (start us, length us, event | category | flops | bytes accessed | tf_op | source)
XLA Modules:
  0.0 87.7 jit_solution(4928081922755396115)
XLA Ops:
  1.3 83.4 %shard_map.85 = (f32[256,256]{1,0:T(8,128)}, f32[256,256]{1,0:T(8,128)}, f32[2,256]{1,0:T(2,128)}) custom-call(s32[16]{0:T(128)} %brow.1, s32[16]{0:T(128)} %bcol.1, s32[1]{0:T(128)S(6)} %copy.12.counts, f32[16,128,128]{2,1,0:T(8,128)} %blocks_hbm.1, f32[2,128]{1,0:T(2,128)} %bitcast.1, f32[256,256]{1,0:T(8,128)} %vec_hbm.1), custom_call_target="tpu_custom_call" | custom-call | tf_op jit(solution)/shard_map/pallas_call | solution.py:355
  84.7 0.0 copy-start
  84.7 1.7 %copy.13 = f32[256,256]{1,0:T(8,128)} copy(f32[256,256]{1,0:T(8,128)} %get-tuple-element.6) | data formatting | bytes 524288
  86.4 0.0 copy-done
  86.4 0.0 copy-start.1
  86.4 0.7 copy.14
  87.1 0.0 copy-done.1
  87.1 0.6 copy.15
Async XLA Ops:
  84.7 1.7 %copy-start = (f32[256,256]{1,0:T(8,128)S(1)}, f32[256,256]{1,0:T(8,128)}, u32[]{:S(2)}) copy-start(f32[256,256]{1,0:T(8,128)} %get-tuple-element.7) | copy-start | bytes 786436
  86.4 0.7 copy-start.1

commit v3 on v2

--- a/solution.py
+++ b/solution.py
@@ -264,7 +264,7 @@
                     w_high[p, pl.ds(j * tile, tile), at] = high * keep
                     w_low[p, pl.ds(j * tile, tile), at] = low * keep
 
-    half = chips // 2
+    half = chips // 2 + 1
     rest = min(chips, chips - half + 1)
     late = max(rest, chips - 1)
     clear(0)

time: 87.9 us -> 89.8 us (1.022)
  Pallas kernels: 83.4 us -> 85.3 us
    pallas_call x1, Pallas kernels: 83.4 us -> 85.3 us  [per_device(): pl.pallas_call(functools.partial(kernel, n_rows, n_cols, mine * n_rows *...]
where the time goes in v3:
time: 89.8 us; the launch traced here: 89.6 us
  Pallas kernels  85.3 us (95%)
  local copies, waits for them, and re-layouts  3 us (3%)
  between operations  1.3 us (1%)
    pallas_call x1, Pallas kernels, per_device(): pl.pallas_call(functools.partial(kernel, n_rows, n_cols, mine * n_rows *...  85.3 us
    unnamed x7, local copies, waits for them, and re-layouts  3 us

profile of v3, /device:TPU:0, one launch (start us, length us, event | category | flops | bytes accessed | tf_op | source)
XLA Modules:
  0.0 89.6 jit_solution(11890236601381170497)
XLA Ops:
  1.3 85.3 %shard_map.85 = (f32[256,256]{1,0:T(8,128)}, f32[256,256]{1,0:T(8,128)}, f32[2,256]{1,0:T(2,128)}) custom-call(s32[16]{0:T(128)} %brow.1, s32[16]{0:T(128)} %bcol.1, s32[1]{0:T(128)S(6)} %copy.12.counts, f32[16,128,128]{2,1,0:T(8,128)} %blocks_hbm.1, f32[2,128]{1,0:T(2,128)} %bitcast.1, f32[256,256]{1,0:T(8,128)} %vec_hbm.1), custom_call_target="tpu_custom_call" | custom-call | tf_op jit(solution)/shard_map/pallas_call | solution.py:355
  86.6 0.0 copy-start
  86.6 1.7 %copy.13 = f32[256,256]{1,0:T(8,128)} copy(f32[256,256]{1,0:T(8,128)} %get-tuple-element.6) | data formatting | bytes 524288
  88.4 0.0 copy-done
  88.4 0.0 copy-start.1
  88.4 0.7 copy.14
  89.1 0.0 copy-done.1
  89.1 0.6 copy.15
Async XLA Ops:
  86.6 1.7 %copy-start = (f32[256,256]{1,0:T(8,128)S(1)}, f32[256,256]{1,0:T(8,128)}, u32[]{:S(2)}) copy-start(f32[256,256]{1,0:T(8,128)} %get-tuple-element.7) | copy-start | bytes 786436
  88.4 0.7 copy-start.1
